TPU v7x, 32 devices: a whole 2x2x4 slice. The times are simulated.
32 devices in a mesh: tm: 4 (over y, x), space: 8 (over z, core).
Axes of the slice: x: 2, y: 2, z: 4, core: 2. Of those that a mesh axis runs over, the one named last changes fastest.
Arguments:
- source: float32 [16, 32, 96, 128], P('tm', 'space'), may hold values from -6 to 6
- initial: float32 [32, 96, 128], P('space'), may hold values from -6 to 6
- mobility: float32 [32, 96, 128], P('space'), may hold values from 0.5 to 2
- labels: int32 [32, 96, 128], P('space'), may hold values from 0 to 3
- electrode: int32 [32, 96, 128], P('space'), may hold values 0 or 1
- rates: float32 [4], replicated, may hold values from 0.2 to 1
Outputs:
- density: float32 [16, 32, 96, 128], P('tm', 'space')
All inputs are finite; a program needn't handle non-finite values. No bound on the sum of `electrode` on one device may be relied on, other than what follows from the above.
Results may differ from a plain program's by a relative error of at most 0.00002.
Values sent between devices are 32-bit elements; how exact they have to be, the bound alone decides.
A program may use at most 64 MiB of HBM per device.

v0:
```python
import jax
import jax.numpy as jnp
from jax import lax
from jax.sharding import PartitionSpec as P

PASSES = 4


source_coef = 0.5
drift_coef = 0.5
react_coef = 0.5
damping = 0.8
coarse_lateral = 0.06
coarse_axial = 0.12


def with_halo(cells, sides, width):
    for axis, dim in sides:
        count = lax.axis_size(axis)
        ends = count - 1
        head = lax.slice_in_dim(cells, 0, width, axis=dim)
        tail = lax.slice_in_dim(cells, cells.shape[dim] - width, cells.shape[dim], axis=dim)
        cells = jnp.concatenate(
            [
                lax.ppermute(tail, axis, [(i, (i + 1) % count) for i in range(ends)]),
                cells,
                lax.ppermute(head, axis, [((i + 1) % count, i) for i in range(ends)]),
            ],
            axis=dim,
        )
    return cells


def passed_along(value, axis, steps):
    count = lax.axis_size(axis)
    first, last = (max(0, -steps), min(count, count - steps))
    return lax.ppermute(value, axis, [(source, source + steps) for source in range(first, last)])


def pad_across(values):
    return jnp.pad(values, ((0, 0), (0, 0), (1, 1), (1, 1)))


def balance(window, mobile, rate_field, forcing):
    current = window[1:, 1:-1]
    former = window[:-1, 1:-1]
    middle = mobile[:, 1:-1]
    spread = pad_across(middle)
    below_x = 0.5 * (middle + mobile[:, :-2])
    above_x = 0.5 * (middle + mobile[:, 2:])
    below_y = 0.5 * (middle + spread[:, :, :-2, 1:-1])
    above_y = 0.5 * (middle + spread[:, :, 2:, 1:-1])
    below_z = 0.5 * (middle + spread[:, :, 1:-1, :-2])
    above_z = 0.5 * (middle + spread[:, :, 1:-1, 2:])
    beside_all = pad_across(current)
    lower_z = beside_all[:, :, 1:-1, :-2]
    summed = below_x + above_x + below_y + above_y + below_z + above_z
    inflow = (
        below_x * window[1:, :-2]
        + above_x * window[1:, 2:]
        + below_y * beside_all[:, :, :-2, 1:-1]
        + above_y * beside_all[:, :, 2:, 1:-1]
        + below_z * lower_z
        + above_z * beside_all[:, :, 1:-1, 2:]
        - summed * current
    )
    carried = below_z * lower_z - above_z * current
    magnitude = jnp.abs(current)
    excess = (
        current
        - former
        - inflow
        - drift_coef * carried
        + react_coef * rate_field * current * magnitude
    )
    residue = forcing - excess
    diagonal = 1.0 + summed + drift_coef * above_z + rate_field * magnitude
    return (residue, diagonal, current)


def relax(window, mobile, rate_field, freedom, forcing):
    residue, diagonal, current = balance(window, mobile, rate_field, forcing)
    updated = current + damping * freedom * residue / diagonal
    return jnp.concatenate([window[:1, 1:-1], updated], axis=0)


def coarse_change(extended, mobility_ext):
    centre = extended[1:-1, 1:-1]
    centre_mob = mobility_ext[1:-1, 1:-1]
    padded_value = jnp.pad(centre, ((0, 0), (0, 0), (1, 1)))
    padded_mob = jnp.pad(centre_mob, ((0, 0), (0, 0), (1, 1)))

    def couple(value_near, mobile_near):
        return 0.5 * (centre_mob + mobile_near) * (value_near - centre)

    lateral = (
        couple(extended[:-2, 1:-1], mobility_ext[:-2, 1:-1])
        + couple(extended[2:, 1:-1], mobility_ext[2:, 1:-1])
        + couple(extended[1:-1, :-2], mobility_ext[1:-1, :-2])
        + couple(extended[1:-1, 2:], mobility_ext[1:-1, 2:])
    )
    along_z = couple(padded_value[:, :, :-2], padded_mob[:, :, :-2]) + couple(
        padded_value[:, :, 2:], padded_mob[:, :, 2:]
    )
    return centre + coarse_lateral * lateral + coarse_axial * along_z


def region_rates(labels, rates):
    matches = labels[None] == jnp.arange(rates.shape[0], dtype=jnp.int32)[:, None, None, None]
    return jnp.sum(jnp.where(matches, rates[:, None, None, None], 0.0), axis=0)


def restrict(residue):
    step_count, planes, across, depth_z = residue.shape
    grouped = residue.reshape(step_count // 4, 4, planes // 2, 2, across // 2, 2, depth_z)
    return 0.25 * jnp.sum(grouped, axis=(1, 3, 5))


def coarse_mobility(mobility):
    planes, across, depth_z = mobility.shape
    return 0.25 * jnp.sum(mobility.reshape(planes // 2, 2, across // 2, 2, depth_z), axis=(1, 3))


def prolong(correction):
    return jnp.repeat(jnp.repeat(jnp.repeat(correction, 4, axis=0), 2, axis=1), 2, axis=2)


def on_device(source, initial, mobility, labels, electrode, rates):
    rate_field = region_rates(labels, rates)[None]
    freedom = (1.0 - electrode.astype(jnp.float32))[None]
    forcing = source_coef * source
    leading = lax.axis_index("tm") == 0
    near_mob = with_halo(mobility[None], (("space", 1),), 1)

    def with_previous(iterate):
        arrived = passed_along(iterate[-1], "tm", 1)
        opening = jnp.where(leading, initial, arrived)
        return jnp.concatenate([opening[None], iterate], axis=0)

    def sweep(iterate):
        window = with_previous(iterate)
        for number in range(PASSES):
            extended = with_halo(window, (("space", 1),), 1)
            window = relax(extended, near_mob, rate_field, freedom, forcing)
        return window[1:]

    iterate = jnp.broadcast_to(initial, source.shape)
    iterate = sweep(iterate)
    extended = with_halo(with_previous(iterate), (("space", 1),), 1)
    residue = balance(extended, near_mob, rate_field, forcing)[0]
    coarse_rhs = restrict(residue)
    coarse_mob = with_halo(coarse_mobility(mobility), (("space", 0),), 1)
    quarter = coarse_rhs.shape[0]
    gathered = lax.all_gather(coarse_rhs, "tm", axis=0, tiled=True)
    mob_ext = jnp.pad(coarse_mob, ((0, 0), (1, 1), (0, 0)))

    def advance(carry_state, forcing_row):
        bordered = with_halo(carry_state, (("space", 0),), 1)
        bordered = jnp.pad(bordered, ((0, 0), (1, 1), (0, 0)))
        advanced = coarse_change(bordered, mob_ext) + forcing_row
        return (advanced, advanced)

    final_state, history = lax.scan(advance, jnp.zeros(gathered.shape[1:], jnp.float32), gathered)
    returned = lax.dynamic_slice_in_dim(history, lax.axis_index("tm") * quarter, quarter, 0)
    iterate = iterate + freedom * prolong(returned)
    iterate = sweep(iterate)
    return iterate


def solution(mesh):
    return jax.shard_map(
        on_device,
        mesh=mesh,
        in_specs=(
            P("tm", "space", None, None),
            P("space", None, None),
            P("space", None, None),
            P("space", None, None),
            P("space", None, None),
            P(),
        ),
        out_specs=P("tm", "space", None, None),
        check_vma=False,
    )
```

profile of v0, /device:TPU:13, one launch (start us, length us, event | category | flops | bytes accessed | tf_op | source)
XLA Modules:
  0.0 195.8 jit_solution(13467515694153484516)
XLA Ops:
  0.9 3.8 %collective-permute-start.3 = (f32[1,1,96,128]{3,2,1,0:T(8,128)S(1)}, f32[1,1,96,128]{3,2,1,0:T(8,128)S(1)}, u32[]{:S(2)}, u32[]{:S(2)}) collective-permute-start(f32[1,1,96,128]{3,2,1,0:T(8,128)S(1)} %get-tuple-element.178), channel_id=1, source_target_pairs={{0,1},{1,2},{2,3},{3,4},{4,5},{5,6},{6,7},{8,9},{9,10},{10,11},{11... | collective-permute-start | bytes 147464 | tf_op jit(solution)/shard_map/ppermute | solution.py:25
  6.6 3.1 %collective-permute-start.2 = (f32[4,96,128]{2,1,0:T(8,128)}, f32[4,96,128]{2,1,0:T(8,128)S(1)}, u32[]{:S(2)}, u32[]{:S(2)}) collective-permute-start(f32[4,96,128]{2,1,0:T(8,128)} %param.9), channel_id=1, source_target_pairs={{0,8},{8,16},{16,24},{1,9},{9,17},{17,25},{2,10},{10,18},{18,26},{... | collective-permute-start | bytes 589832 | tf_op jit(solution)/shard_map/ppermute | solution.py:37
  12.0 3.5 %collective-permute-done.2 = f32[4,96,128]{2,1,0:T(8,128)S(1)} collective-permute-done((f32[4,96,128]{2,1,0:T(8,128)}, f32[4,96,128]{2,1,0:T(8,128)S(1)}, u32[]{:S(2)}, u32[]{:S(2)}) %collective-permute-start.2) | collective-permute-done | bytes 196640 | tf_op jit(solution)/shard_map/ppermute | solution.py:37
  15.8 4.6 %collective-permute-start.4 = (f32[5,1,96,128]{3,2,1,0:T(8,128)S(1)}, f32[5,1,96,128]{3,2,1,0:T(8,128)S(1)}, u32[]{:S(2)}, u32[]{:S(2)}) collective-permute-start(f32[5,1,96,128]{3,2,1,0:T(8,128)S(1)} %get-tuple-element.166), channel_id=1, source_target_pairs={{0,1},{1,2},{2,3},{3,4},{4,5},{5,6},{6,7},{8,9},{9,10},{10,11},{11... | collective-permute-start | bytes 737288 | tf_op jit(solution)/shard_map/ppermute | solution.py:25
  23.6 4.4 %collective-permute-done.6 = f32[5,1,96,128]{3,2,1,0:T(8,128)S(1)} collective-permute-done((f32[5,1,96,128]{3,2,1,0:T(8,128)S(1)}, f32[5,1,96,128]{3,2,1,0:T(8,128)S(1)}, u32[]{:S(2)}, u32[]{:S(2)}) %collective-permute-start.6) | collective-permute-done | bytes 245792 | tf_op jit(solution)/shard_map/ppermute | solution.py:27
  30.8 2.4 %collective-permute-start.8 = (f32[5,1,96,128]{3,2,1,0:T(8,128)S(1)}, f32[5,1,96,128]{3,2,1,0:T(8,128)S(1)}, u32[]{:S(2)}, u32[]{:S(2)}) collective-permute-start(f32[5,1,96,128]{3,2,1,0:T(8,128)S(1)} %get-tuple-element.165), channel_id=1, source_target_pairs={{1,0},{2,1},{3,2},{4,3},{5,4},{6,5},{7,6},{9,8},{10,9},{11,10},{12... | collective-permute-start | bytes 737288 | tf_op jit(solution)/shard_map/ppermute | solution.py:27
  34.0 4.4 %collective-permute-done.8 = f32[5,1,96,128]{3,2,1,0:T(8,128)S(1)} collective-permute-done((f32[5,1,96,128]{3,2,1,0:T(8,128)S(1)}, f32[5,1,96,128]{3,2,1,0:T(8,128)S(1)}, u32[]{:S(2)}, u32[]{:S(2)}) %collective-permute-start.8) | collective-permute-done | bytes 245792 | tf_op jit(solution)/shard_map/ppermute | solution.py:27
  41.4 3.6 %collective-permute-start.9 = (f32[5,1,96,128]{3,2,1,0:T(8,128)S(1)}, f32[5,1,96,128]{3,2,1,0:T(8,128)S(1)}, u32[]{:S(2)}, u32[]{:S(2)}) collective-permute-start(f32[5,1,96,128]{3,2,1,0:T(8,128)S(1)} %get-tuple-element.162), channel_id=1, source_target_pairs={{0,1},{1,2},{2,3},{3,4},{4,5},{5,6},{6,7},{8,9},{9,10},{10,11},{11... | collective-permute-start | bytes 737288 | tf_op jit(solution)/shard_map/ppermute | solution.py:25
  50.8 4.4 %collective-permute-start.11 = (f32[5,1,96,128]{3,2,1,0:T(8,128)}, f32[5,1,96,128]{3,2,1,0:T(8,128)}, u32[]{:S(2)}, u32[]{:S(2)}) collective-permute-start(f32[5,1,96,128]{3,2,1,0:T(8,128)} %get-tuple-element.160), channel_id=1, source_target_pairs={{0,1},{1,2},{2,3},{3,4},{4,5},{5,6},{6,7},{8,9},{9,10},{10,11},{11... | collective-permute-start | bytes 737288 | tf_op jit(solution)/shard_map/ppermute | solution.py:25
  58.7 4.3 %collective-permute-done.12 = f32[5,1,96,128]{3,2,1,0:T(8,128)} collective-permute-done((f32[5,1,96,128]{3,2,1,0:T(8,128)}, f32[5,1,96,128]{3,2,1,0:T(8,128)}, u32[]{:S(2)}, u32[]{:S(2)}) %collective-permute-start.12) | collective-permute-done | bytes 245792 | tf_op jit(solution)/shard_map/ppermute | solution.py:27
  63.1 4.9 %fusion.75 = f32[4,4,96,128]{3,2,1,0:T(8,128)S(1)} fusion(f32[4,4,96,128]{3,2,1,0:T(8,128)} %copy-done.4, f32[1,4,96,128]{3,2,1,0:T(8,128)S(1)} %get-tuple-element.177, f32[5,1,96,128]{3,2,1,0:T(8,128)} %collective-permute-done.12, f32[5,1,96,128]{3,2,1,0:T(8,128)} %collective-permute-done.11, f32[4,4,96,128]{3,2,1,0:T(8,128)S(1)} %copy-done, ...), kind=kLoop, calls=%fused_computation.165 | loop fusion | flops 6881280 | bytes 5210112 | tf_op jit(solution)/shard_map/add | solution.py:83
  79.6 3.6 %collective-permute-start.16 = (f32[5,1,96,128]{3,2,1,0:T(8,128)S(1)}, f32[5,1,96,128]{3,2,1,0:T(8,128)S(1)}, u32[]{:S(2)}, u32[]{:S(2)}) collective-permute-start(f32[5,1,96,128]{3,2,1,0:T(8,128)S(1)} %get-tuple-element.158), channel_id=1, source_target_pairs={{0,1},{1,2},{2,3},{3,4},{4,5},{5,6},{6,7},{8,9},{9,10},{10,11},{11... | collective-permute-start | bytes 737288 | tf_op jit(solution)/shard_map/ppermute | solution.py:25
  86.6 4.1 %collective-permute-done.17 = f32[5,1,96,128]{3,2,1,0:T(8,128)S(1)} collective-permute-done((f32[5,1,96,128]{3,2,1,0:T(8,128)S(1)}, f32[5,1,96,128]{3,2,1,0:T(8,128)S(1)}, u32[]{:S(2)}, u32[]{:S(2)}) %collective-permute-start.17) | collective-permute-done | bytes 245792 | tf_op jit(solution)/shard_map/ppermute | solution.py:27
  93.4 6.7 %all-gather = f32[8,48,128]{2,1,0:T(8,128)} all-gather(f32[2,48,128]{2,1,0:T(8,128)S(1)} %broadcast_multiply_fusion.1), channel_id=2, replica_groups=mesh['tm'=4,'space'=8] {'tm'}, dimensions={0}, use_global_device_ids=true | all-gather | bytes 245760 | tf_op jit(solution)/shard_map/all_gather | solution.py:154
  100.1 39.9 %while.15 = (s32[]{:T(128)}, f32[2,48,128]{2,1,0:T(8,128)}, f32[4,2,48,128]{3,2,1,0:T(8,128)}, f32[2,48,128]{2,1,0:T(8,128)S(1)}, f32[2,48,128]{2,1,0:T(8,128)},...) while((s32[]{:T(128)}, f32[2,48,128]{2,1,0:T(8,128)}, ...), condition=%wide.region_5.6_spmd.clone, body=%wide.region_4.5_spmd.clone.sunk | while | flops 598019 | bytes 1282259 | solution.py:163
  102.6 3.6 %collective-permute-start.1 = (f32[1,48,128]{2,1,0:T(8,128)}, f32[1,48,128]{2,1,0:T(8,128)S(1)}, u32[]{:S(2)}, u32[]{:S(2)}) collective-permute-start(f32[1,48,128]{2,1,0:T(8,128)} %get-tuple-element.248), channel_id=1, source_target_pairs={{0,1},{1,2},{2,3},{3,4},{4,5},{5,6},{6,7},{8,9},{9,10},{10,11},{11... | collective-permute-start | bytes 73736 | tf_op jit(solution)/shard_map/while/body/eval_jaxpr/ppermute | solution.py:25
  110.5 2.7 %collective-permute-start = (f32[1,48,128]{2,1,0:T(8,128)}, f32[1,48,128]{2,1,0:T(8,128)S(1)}, u32[]{:S(2)}, u32[]{:S(2)}) collective-permute-start(f32[1,48,128]{2,1,0:T(8,128)} %get-tuple-element.247), channel_id=1, source_target_pairs={{1,0},{2,1},{3,2},{4,3},{5,4},{6,5},{7,6},{9,8},{10,9},{11,10},{12... | collective-permute-start | bytes 73736 | tf_op jit(solution)/shard_map/while/body/eval_jaxpr/ppermute | solution.py:27
  113.2 3.4 %collective-permute-start.1 = (f32[1,48,128]{2,1,0:T(8,128)}, f32[1,48,128]{2,1,0:T(8,128)S(1)}, u32[]{:S(2)}, u32[]{:S(2)}) collective-permute-start(f32[1,48,128]{2,1,0:T(8,128)} %get-tuple-element.248), channel_id=1, source_target_pairs={{0,1},{1,2},{2,3},{3,4},{4,5},{5,6},{6,7},{8,9},{9,10},{10,11},{11... | collective-permute-start | bytes 73736 | tf_op jit(solution)/shard_map/while/body/eval_jaxpr/ppermute | solution.py:25
  120.8 2.7 %collective-permute-start = (f32[1,48,128]{2,1,0:T(8,128)}, f32[1,48,128]{2,1,0:T(8,128)S(1)}, u32[]{:S(2)}, u32[]{:S(2)}) collective-permute-start(f32[1,48,128]{2,1,0:T(8,128)} %get-tuple-element.247), channel_id=1, source_target_pairs={{1,0},{2,1},{3,2},{4,3},{5,4},{6,5},{7,6},{9,8},{10,9},{11,10},{12... | collective-permute-start | bytes 73736 | tf_op jit(solution)/shard_map/while/body/eval_jaxpr/ppermute | solution.py:27
  123.5 3.4 %collective-permute-start.1 = (f32[1,48,128]{2,1,0:T(8,128)}, f32[1,48,128]{2,1,0:T(8,128)S(1)}, u32[]{:S(2)}, u32[]{:S(2)}) collective-permute-start(f32[1,48,128]{2,1,0:T(8,128)} %get-tuple-element.248), channel_id=1, source_target_pairs={{0,1},{1,2},{2,3},{3,4},{4,5},{5,6},{6,7},{8,9},{9,10},{10,11},{11... | collective-permute-start | bytes 73736 | tf_op jit(solution)/shard_map/while/body/eval_jaxpr/ppermute | solution.py:25
  131.1 2.7 %collective-permute-start = (f32[1,48,128]{2,1,0:T(8,128)}, f32[1,48,128]{2,1,0:T(8,128)S(1)}, u32[]{:S(2)}, u32[]{:S(2)}) collective-permute-start(f32[1,48,128]{2,1,0:T(8,128)} %get-tuple-element.247), channel_id=1, source_target_pairs={{1,0},{2,1},{3,2},{4,3},{5,4},{6,5},{7,6},{9,8},{10,9},{11,10},{12... | collective-permute-start | bytes 73736 | tf_op jit(solution)/shard_map/while/body/eval_jaxpr/ppermute | solution.py:27
  133.8 3.4 %collective-permute-start.1 = (f32[1,48,128]{2,1,0:T(8,128)}, f32[1,48,128]{2,1,0:T(8,128)S(1)}, u32[]{:S(2)}, u32[]{:S(2)}) collective-permute-start(f32[1,48,128]{2,1,0:T(8,128)} %get-tuple-element.248), channel_id=1, source_target_pairs={{0,1},{1,2},{2,3},{3,4},{4,5},{5,6},{6,7},{8,9},{9,10},{10,11},{11... | collective-permute-start | bytes 73736 | tf_op jit(solution)/shard_map/while/body/eval_jaxpr/ppermute | solution.py:25
  142.1 2.9 %collective-permute-start.18 = (f32[4,96,128]{2,1,0:T(8,128)S(1)}, f32[4,96,128]{2,1,0:T(8,128)S(1)}, u32[]{:S(2)}, u32[]{:S(2)}) collective-permute-start(f32[4,96,128]{2,1,0:T(8,128)S(1)} %slice_bitcast_fusion), channel_id=1, source_target_pairs={{0,8},{8,16},{16,24},{1,9},{9,17},{17,25},{2,10},{10,18},{18,26},{... | collective-permute-start | bytes 589832 | tf_op jit(solution)/shard_map/ppermute | solution.py:37
  145.0 5.5 %collective-permute-done.18 = f32[4,96,128]{2,1,0:T(8,128)S(1)} collective-permute-done((f32[4,96,128]{2,1,0:T(8,128)S(1)}, f32[4,96,128]{2,1,0:T(8,128)S(1)}, u32[]{:S(2)}, u32[]{:S(2)}) %collective-permute-start.18) | collective-permute-done | bytes 196640 | tf_op jit(solution)/shard_map/ppermute | solution.py:37
  150.6 4.2 %collective-permute-start.19 = (f32[5,1,96,128]{3,2,1,0:T(8,128)S(1)}, f32[5,1,96,128]{3,2,1,0:T(8,128)S(1)}, u32[]{:S(2)}, u32[]{:S(2)}) collective-permute-start(f32[5,1,96,128]{3,2,1,0:T(8,128)S(1)} %get-tuple-element.156), channel_id=1, source_target_pairs={{0,1},{1,2},{2,3},{3,4},{4,5},{5,6},{6,7},{8,9},{9,10},{10,11},{11... | collective-permute-start | bytes 737288 | tf_op jit(solution)/shard_map/ppermute | solution.py:25
  157.9 4.4 %collective-permute-done.20 = f32[5,1,96,128]{3,2,1,0:T(8,128)S(1)} collective-permute-done((f32[5,1,96,128]{3,2,1,0:T(8,128)S(1)}, f32[5,1,96,128]{3,2,1,0:T(8,128)S(1)}, u32[]{:S(2)}, u32[]{:S(2)}) %collective-permute-start.20) | collective-permute-done | bytes 245792 | tf_op jit(solution)/shard_map/ppermute | solution.py:27
  165.3 2.4 %collective-permute-start.22 = (f32[5,1,96,128]{3,2,1,0:T(8,128)S(1)}, f32[5,1,96,128]{3,2,1,0:T(8,128)S(1)}, u32[]{:S(2)}, u32[]{:S(2)}) collective-permute-start(f32[5,1,96,128]{3,2,1,0:T(8,128)S(1)} %get-tuple-element.155), channel_id=1, source_target_pairs={{1,0},{2,1},{3,2},{4,3},{5,4},{6,5},{7,6},{9,8},{10,9},{11,10},{12... | collective-permute-start | bytes 737288 | tf_op jit(solution)/shard_map/ppermute | solution.py:27
  168.4 4.4 %collective-permute-done.22 = f32[5,1,96,128]{3,2,1,0:T(8,128)S(1)} collective-permute-done((f32[5,1,96,128]{3,2,1,0:T(8,128)S(1)}, f32[5,1,96,128]{3,2,1,0:T(8,128)S(1)}, u32[]{:S(2)}, u32[]{:S(2)}) %collective-permute-start.22) | collective-permute-done | bytes 245792 | tf_op jit(solution)/shard_map/ppermute | solution.py:27
  175.8 2.4 %collective-permute-start.24 = (f32[5,1,96,128]{3,2,1,0:T(8,128)S(1)}, f32[5,1,96,128]{3,2,1,0:T(8,128)S(1)}, u32[]{:S(2)}, u32[]{:S(2)}) collective-permute-start(f32[5,1,96,128]{3,2,1,0:T(8,128)S(1)} %get-tuple-element.153), channel_id=1, source_target_pairs={{1,0},{2,1},{3,2},{4,3},{5,4},{6,5},{7,6},{9,8},{10,9},{11,10},{12... | collective-permute-start | bytes 737288 | tf_op jit(solution)/shard_map/ppermute | solution.py:27
  179.0 4.4 %collective-permute-done.24 = f32[5,1,96,128]{3,2,1,0:T(8,128)S(1)} collective-permute-done((f32[5,1,96,128]{3,2,1,0:T(8,128)S(1)}, f32[5,1,96,128]{3,2,1,0:T(8,128)S(1)}, u32[]{:S(2)}, u32[]{:S(2)}) %collective-permute-start.24) | collective-permute-done | bytes 245792 | tf_op jit(solution)/shard_map/ppermute | solution.py:27
  186.3 2.4 %collective-permute-start.26 = (f32[5,1,96,128]{3,2,1,0:T(8,128)S(1)}, f32[5,1,96,128]{3,2,1,0:T(8,128)S(1)}, u32[]{:S(2)}, u32[]{:S(2)}) collective-permute-start(f32[5,1,96,128]{3,2,1,0:T(8,128)S(1)} %get-tuple-element.151), channel_id=1, source_target_pairs={{1,0},{2,1},{3,2},{4,3},{5,4},{6,5},{7,6},{9,8},{10,9},{11,10},{12... | collective-permute-start | bytes 737288 | tf_op jit(solution)/shard_map/ppermute | solution.py:27
  189.5 4.4 %collective-permute-done.26 = f32[5,1,96,128]{3,2,1,0:T(8,128)S(1)} collective-permute-done((f32[5,1,96,128]{3,2,1,0:T(8,128)S(1)}, f32[5,1,96,128]{3,2,1,0:T(8,128)S(1)}, u32[]{:S(2)}, u32[]{:S(2)}) %collective-permute-start.26) | collective-permute-done | bytes 245792 | tf_op jit(solution)/shard_map/ppermute | solution.py:27
  (125 shorter events, 77.9 us)
Async XLA Ops:
  0.9 10.9 %collective-permute-start.3 = (f32[1,1,96,128]{3,2,1,0:T(8,128)S(1)}, f32[1,1,96,128]{3,2,1,0:T(8,128)S(1)}, u32[]{:S(2)}, u32[]{:S(2)}) collective-permute-start(f32[1,1,96,128]{3,2,1,0:T(8,128)S(1)} %get-tuple-element.178), channel_id=1, source_target_pairs={{0,1},{1,2},{2,3},{3,4},{4,5},{5,6},{6,7},{8,9},{9,10},{10,11},{11... | collective-permute-start | bytes 147464 | tf_op jit(solution)/shard_map/ppermute | solution.py:25
  4.7 7.2 %collective-permute-start.5 = (f32[1,1,96,128]{3,2,1,0:T(8,128)S(1)}, f32[1,1,96,128]{3,2,1,0:T(8,128)S(1)}, u32[]{:S(2)}, u32[]{:S(2)}) collective-permute-start(f32[1,1,96,128]{3,2,1,0:T(8,128)S(1)} %get-tuple-element.179), channel_id=1, source_target_pairs={{1,0},{2,1},{3,2},{4,3},{5,4},{6,5},{7,6},{9,8},{10,9},{11,10},{12... | collective-permute-start | bytes 147464 | tf_op jit(solution)/shard_map/ppermute | solution.py:27
  6.6 8.9 %collective-permute-start.2 = (f32[4,96,128]{2,1,0:T(8,128)}, f32[4,96,128]{2,1,0:T(8,128)S(1)}, u32[]{:S(2)}, u32[]{:S(2)}) collective-permute-start(f32[4,96,128]{2,1,0:T(8,128)} %param.9), channel_id=1, source_target_pairs={{0,8},{8,16},{16,24},{1,9},{9,17},{17,25},{2,10},{10,18},{18,26},{... | collective-permute-start | bytes 589832 | tf_op jit(solution)/shard_map/ppermute | solution.py:37
  15.8 7.8 %collective-permute-start.4 = (f32[5,1,96,128]{3,2,1,0:T(8,128)S(1)}, f32[5,1,96,128]{3,2,1,0:T(8,128)S(1)}, u32[]{:S(2)}, u32[]{:S(2)}) collective-permute-start(f32[5,1,96,128]{3,2,1,0:T(8,128)S(1)} %get-tuple-element.166), channel_id=1, source_target_pairs={{0,1},{1,2},{2,3},{3,4},{4,5},{5,6},{6,7},{8,9},{9,10},{10,11},{11... | collective-permute-start | bytes 737288 | tf_op jit(solution)/shard_map/ppermute | solution.py:25
  20.5 7.5 %collective-permute-start.6 = (f32[5,1,96,128]{3,2,1,0:T(8,128)S(1)}, f32[5,1,96,128]{3,2,1,0:T(8,128)S(1)}, u32[]{:S(2)}, u32[]{:S(2)}) collective-permute-start(f32[5,1,96,128]{3,2,1,0:T(8,128)S(1)} %get-tuple-element.167), channel_id=1, source_target_pairs={{1,0},{2,1},{3,2},{4,3},{5,4},{6,5},{7,6},{9,8},{10,9},{11,10},{12... | collective-permute-start | bytes 737288 | tf_op jit(solution)/shard_map/ppermute | solution.py:27
  28.9 5.0 %collective-permute-start.7 = (f32[5,1,96,128]{3,2,1,0:T(8,128)S(1)}, f32[5,1,96,128]{3,2,1,0:T(8,128)S(1)}, u32[]{:S(2)}, u32[]{:S(2)}) collective-permute-start(f32[5,1,96,128]{3,2,1,0:T(8,128)S(1)} %get-tuple-element.164), channel_id=1, source_target_pairs={{0,1},{1,2},{2,3},{3,4},{4,5},{5,6},{6,7},{8,9},{9,10},{10,11},{11... | collective-permute-start | bytes 737288 | tf_op jit(solution)/shard_map/ppermute | solution.py:25
  30.8 7.5 %collective-permute-start.8 = (f32[5,1,96,128]{3,2,1,0:T(8,128)S(1)}, f32[5,1,96,128]{3,2,1,0:T(8,128)S(1)}, u32[]{:S(2)}, u32[]{:S(2)}) collective-permute-start(f32[5,1,96,128]{3,2,1,0:T(8,128)S(1)} %get-tuple-element.165), channel_id=1, source_target_pairs={{1,0},{2,1},{3,2},{4,3},{5,4},{6,5},{7,6},{9,8},{10,9},{11,10},{12... | collective-permute-start | bytes 737288 | tf_op jit(solution)/shard_map/ppermute | solution.py:27
  39.4 7.8 %collective-permute-start.10 = (f32[5,1,96,128]{3,2,1,0:T(8,128)S(1)}, f32[5,1,96,128]{3,2,1,0:T(8,128)S(1)}, u32[]{:S(2)}, u32[]{:S(2)}) collective-permute-start(f32[5,1,96,128]{3,2,1,0:T(8,128)S(1)} %get-tuple-element.163), channel_id=1, source_target_pairs={{1,0},{2,1},{3,2},{4,3},{5,4},{6,5},{7,6},{9,8},{10,9},{11,10},{12... | collective-permute-start | bytes 737288 | tf_op jit(solution)/shard_map/ppermute | solution.py:27
  41.4 6.8 %collective-permute-start.9 = (f32[5,1,96,128]{3,2,1,0:T(8,128)S(1)}, f32[5,1,96,128]{3,2,1,0:T(8,128)S(1)}, u32[]{:S(2)}, u32[]{:S(2)}) collective-permute-start(f32[5,1,96,128]{3,2,1,0:T(8,128)S(1)} %get-tuple-element.162), channel_id=1, source_target_pairs={{0,1},{1,2},{2,3},{3,4},{4,5},{5,6},{6,7},{8,9},{9,10},{10,11},{11... | collective-permute-start | bytes 737288 | tf_op jit(solution)/shard_map/ppermute | solution.py:25
  50.8 7.9 %collective-permute-start.11 = (f32[5,1,96,128]{3,2,1,0:T(8,128)}, f32[5,1,96,128]{3,2,1,0:T(8,128)}, u32[]{:S(2)}, u32[]{:S(2)}) collective-permute-start(f32[5,1,96,128]{3,2,1,0:T(8,128)} %get-tuple-element.160), channel_id=1, source_target_pairs={{0,1},{1,2},{2,3},{3,4},{4,5},{5,6},{6,7},{8,9},{9,10},{10,11},{11... | collective-permute-start | bytes 737288 | tf_op jit(solution)/shard_map/ppermute | solution.py:25
  55.2 7.8 %collective-permute-start.12 = (f32[5,1,96,128]{3,2,1,0:T(8,128)}, f32[5,1,96,128]{3,2,1,0:T(8,128)}, u32[]{:S(2)}, u32[]{:S(2)}) collective-permute-start(f32[5,1,96,128]{3,2,1,0:T(8,128)} %get-tuple-element.161), channel_id=1, source_target_pairs={{1,0},{2,1},{3,2},{4,3},{5,4},{6,5},{7,6},{9,8},{10,9},{11,10},{12... | collective-permute-start | bytes 737288 | tf_op jit(solution)/shard_map/ppermute | solution.py:27
  68.8 8.6 %collective-permute-start.15 = (f32[4,96,128]{2,1,0:T(8,128)S(1)}, f32[4,96,128]{2,1,0:T(8,128)}, u32[]{:S(2)}, u32[]{:S(2)}) collective-permute-start(f32[4,96,128]{2,1,0:T(8,128)S(1)} %slice_bitcast_fusion.1), channel_id=1, source_target_pairs={{0,8},{8,16},{16,24},{1,9},{9,17},{17,25},{2,10},{10,18},{18,26},{... | collective-permute-start | bytes 589832 | tf_op jit(solution)/shard_map/ppermute | solution.py:37
  71.1 14.0 %collective-permute-start.13 = (f32[1,48,128]{2,1,0:T(8,128)S(1)}, f32[1,48,128]{2,1,0:T(8,128)S(1)}, u32[]{:S(2)}, u32[]{:S(2)}) collective-permute-start(f32[1,48,128]{2,1,0:T(8,128)S(1)} %get-tuple-element.185), channel_id=1, source_target_pairs={{0,1},{1,2},{2,3},{3,4},{4,5},{5,6},{6,7},{8,9},{9,10},{10,11},{11... | collective-permute-start | bytes 73736 | tf_op jit(solution)/shard_map/ppermute | solution.py:25
  73.1 12.0 %collective-permute-start.14 = (f32[1,48,128]{2,1,0:T(8,128)S(1)}, f32[1,48,128]{2,1,0:T(8,128)S(1)}, u32[]{:S(2)}, u32[]{:S(2)}) collective-permute-start(f32[1,48,128]{2,1,0:T(8,128)S(1)} %get-tuple-element.184), channel_id=1, source_target_pairs={{1,0},{2,1},{3,2},{4,3},{5,4},{6,5},{7,6},{9,8},{10,9},{11,10},{12... | collective-permute-start | bytes 73736 | tf_op jit(solution)/shard_map/ppermute | solution.py:27
  79.6 7.0 %collective-permute-start.16 = (f32[5,1,96,128]{3,2,1,0:T(8,128)S(1)}, f32[5,1,96,128]{3,2,1,0:T(8,128)S(1)}, u32[]{:S(2)}, u32[]{:S(2)}) collective-permute-start(f32[5,1,96,128]{3,2,1,0:T(8,128)S(1)} %get-tuple-element.158), channel_id=1, source_target_pairs={{0,1},{1,2},{2,3},{3,4},{4,5},{5,6},{6,7},{8,9},{9,10},{10,11},{11... | collective-permute-start | bytes 737288 | tf_op jit(solution)/shard_map/ppermute | solution.py:25
  83.2 7.5 %collective-permute-start.17 = (f32[5,1,96,128]{3,2,1,0:T(8,128)S(1)}, f32[5,1,96,128]{3,2,1,0:T(8,128)S(1)}, u32[]{:S(2)}, u32[]{:S(2)}) collective-permute-start(f32[5,1,96,128]{3,2,1,0:T(8,128)S(1)} %get-tuple-element.159), channel_id=1, source_target_pairs={{1,0},{2,1},{3,2},{4,3},{5,4},{6,5},{7,6},{9,8},{10,9},{11,10},{12... | collective-permute-start | bytes 737288 | tf_op jit(solution)/shard_map/ppermute | solution.py:27
  100.7 5.6 %collective-permute-start = (f32[1,48,128]{2,1,0:T(8,128)}, f32[1,48,128]{2,1,0:T(8,128)S(1)}, u32[]{:S(2)}, u32[]{:S(2)}) collective-permute-start(f32[1,48,128]{2,1,0:T(8,128)} %get-tuple-element.247), channel_id=1, source_target_pairs={{1,0},{2,1},{3,2},{4,3},{5,4},{6,5},{7,6},{9,8},{10,9},{11,10},{12... | collective-permute-start | bytes 73736 | tf_op jit(solution)/shard_map/while/body/eval_jaxpr/ppermute | solution.py:27
  102.6 4.8 %collective-permute-start.1 = (f32[1,48,128]{2,1,0:T(8,128)}, f32[1,48,128]{2,1,0:T(8,128)S(1)}, u32[]{:S(2)}, u32[]{:S(2)}) collective-permute-start(f32[1,48,128]{2,1,0:T(8,128)} %get-tuple-element.248), channel_id=1, source_target_pairs={{0,1},{1,2},{2,3},{3,4},{4,5},{5,6},{6,7},{8,9},{9,10},{10,11},{11... | collective-permute-start | bytes 73736 | tf_op jit(solution)/shard_map/while/body/eval_jaxpr/ppermute | solution.py:25
  110.5 6.2 %collective-permute-start = (f32[1,48,128]{2,1,0:T(8,128)}, f32[1,48,128]{2,1,0:T(8,128)S(1)}, u32[]{:S(2)}, u32[]{:S(2)}) collective-permute-start(f32[1,48,128]{2,1,0:T(8,128)} %get-tuple-element.247), channel_id=1, source_target_pairs={{1,0},{2,1},{3,2},{4,3},{5,4},{6,5},{7,6},{9,8},{10,9},{11,10},{12... | collective-permute-start | bytes 73736 | tf_op jit(solution)/shard_map/while/body/eval_jaxpr/ppermute | solution.py:27
  120.8 6.2 %collective-permute-start = (f32[1,48,128]{2,1,0:T(8,128)}, f32[1,48,128]{2,1,0:T(8,128)S(1)}, u32[]{:S(2)}, u32[]{:S(2)}) collective-permute-start(f32[1,48,128]{2,1,0:T(8,128)} %get-tuple-element.247), channel_id=1, source_target_pairs={{1,0},{2,1},{3,2},{4,3},{5,4},{6,5},{7,6},{9,8},{10,9},{11,10},{12... | collective-permute-start | bytes 73736 | tf_op jit(solution)/shard_map/while/body/eval_jaxpr/ppermute | solution.py:27
  123.5 4.6 %collective-permute-start.1 = (f32[1,48,128]{2,1,0:T(8,128)}, f32[1,48,128]{2,1,0:T(8,128)S(1)}, u32[]{:S(2)}, u32[]{:S(2)}) collective-permute-start(f32[1,48,128]{2,1,0:T(8,128)} %get-tuple-element.248), channel_id=1, source_target_pairs={{0,1},{1,2},{2,3},{3,4},{4,5},{5,6},{6,7},{8,9},{9,10},{10,11},{11... | collective-permute-start | bytes 73736 | tf_op jit(solution)/shard_map/while/body/eval_jaxpr/ppermute | solution.py:25
  131.1 6.2 %collective-permute-start = (f32[1,48,128]{2,1,0:T(8,128)}, f32[1,48,128]{2,1,0:T(8,128)S(1)}, u32[]{:S(2)}, u32[]{:S(2)}) collective-permute-start(f32[1,48,128]{2,1,0:T(8,128)} %get-tuple-element.247), channel_id=1, source_target_pairs={{1,0},{2,1},{3,2},{4,3},{5,4},{6,5},{7,6},{9,8},{10,9},{11,10},{12... | collective-permute-start | bytes 73736 | tf_op jit(solution)/shard_map/while/body/eval_jaxpr/ppermute | solution.py:27
  133.8 4.6 %collective-permute-start.1 = (f32[1,48,128]{2,1,0:T(8,128)}, f32[1,48,128]{2,1,0:T(8,128)S(1)}, u32[]{:S(2)}, u32[]{:S(2)}) collective-permute-start(f32[1,48,128]{2,1,0:T(8,128)} %get-tuple-element.248), channel_id=1, source_target_pairs={{0,1},{1,2},{2,3},{3,4},{4,5},{5,6},{6,7},{8,9},{9,10},{10,11},{11... | collective-permute-start | bytes 73736 | tf_op jit(solution)/shard_map/while/body/eval_jaxpr/ppermute | solution.py:25
  142.1 8.4 %collective-permute-start.18 = (f32[4,96,128]{2,1,0:T(8,128)S(1)}, f32[4,96,128]{2,1,0:T(8,128)S(1)}, u32[]{:S(2)}, u32[]{:S(2)}) collective-permute-start(f32[4,96,128]{2,1,0:T(8,128)S(1)} %slice_bitcast_fusion), channel_id=1, source_target_pairs={{0,8},{8,16},{16,24},{1,9},{9,17},{17,25},{2,10},{10,18},{18,26},{... | collective-permute-start | bytes 589832 | tf_op jit(solution)/shard_map/ppermute | solution.py:37
  150.6 7.4 %collective-permute-start.19 = (f32[5,1,96,128]{3,2,1,0:T(8,128)S(1)}, f32[5,1,96,128]{3,2,1,0:T(8,128)S(1)}, u32[]{:S(2)}, u32[]{:S(2)}) collective-permute-start(f32[5,1,96,128]{3,2,1,0:T(8,128)S(1)} %get-tuple-element.156), channel_id=1, source_target_pairs={{0,1},{1,2},{2,3},{3,4},{4,5},{5,6},{6,7},{8,9},{9,10},{10,11},{11... | collective-permute-start | bytes 737288 | tf_op jit(solution)/shard_map/ppermute | solution.py:25
  154.8 7.5 %collective-permute-start.20 = (f32[5,1,96,128]{3,2,1,0:T(8,128)S(1)}, f32[5,1,96,128]{3,2,1,0:T(8,128)S(1)}, u32[]{:S(2)}, u32[]{:S(2)}) collective-permute-start(f32[5,1,96,128]{3,2,1,0:T(8,128)S(1)} %get-tuple-element.157), channel_id=1, source_target_pairs={{1,0},{2,1},{3,2},{4,3},{5,4},{6,5},{7,6},{9,8},{10,9},{11,10},{12... | collective-permute-start | bytes 737288 | tf_op jit(solution)/shard_map/ppermute | solution.py:27
  163.4 5.0 %collective-permute-start.21 = (f32[5,1,96,128]{3,2,1,0:T(8,128)S(1)}, f32[5,1,96,128]{3,2,1,0:T(8,128)S(1)}, u32[]{:S(2)}, u32[]{:S(2)}) collective-permute-start(f32[5,1,96,128]{3,2,1,0:T(8,128)S(1)} %get-tuple-element.154), channel_id=1, source_target_pairs={{0,1},{1,2},{2,3},{3,4},{4,5},{5,6},{6,7},{8,9},{9,10},{10,11},{11... | collective-permute-start | bytes 737288 | tf_op jit(solution)/shard_map/ppermute | solution.py:25
  165.3 7.5 %collective-permute-start.22 = (f32[5,1,96,128]{3,2,1,0:T(8,128)S(1)}, f32[5,1,96,128]{3,2,1,0:T(8,128)S(1)}, u32[]{:S(2)}, u32[]{:S(2)}) collective-permute-start(f32[5,1,96,128]{3,2,1,0:T(8,128)S(1)} %get-tuple-element.155), channel_id=1, source_target_pairs={{1,0},{2,1},{3,2},{4,3},{5,4},{6,5},{7,6},{9,8},{10,9},{11,10},{12... | collective-permute-start | bytes 737288 | tf_op jit(solution)/shard_map/ppermute | solution.py:27
  173.9 5.0 %collective-permute-start.23 = (f32[5,1,96,128]{3,2,1,0:T(8,128)S(1)}, f32[5,1,96,128]{3,2,1,0:T(8,128)S(1)}, u32[]{:S(2)}, u32[]{:S(2)}) collective-permute-start(f32[5,1,96,128]{3,2,1,0:T(8,128)S(1)} %get-tuple-element.152), channel_id=1, source_target_pairs={{0,1},{1,2},{2,3},{3,4},{4,5},{5,6},{6,7},{8,9},{9,10},{10,11},{11... | collective-permute-start | bytes 737288 | tf_op jit(solution)/shard_map/ppermute | solution.py:25
  175.8 7.5 %collective-permute-start.24 = (f32[5,1,96,128]{3,2,1,0:T(8,128)S(1)}, f32[5,1,96,128]{3,2,1,0:T(8,128)S(1)}, u32[]{:S(2)}, u32[]{:S(2)}) collective-permute-start(f32[5,1,96,128]{3,2,1,0:T(8,128)S(1)} %get-tuple-element.153), channel_id=1, source_target_pairs={{1,0},{2,1},{3,2},{4,3},{5,4},{6,5},{7,6},{9,8},{10,9},{11,10},{12... | collective-permute-start | bytes 737288 | tf_op jit(solution)/shard_map/ppermute | solution.py:27
  184.4 5.0 %collective-permute-start.25 = (f32[5,1,96,128]{3,2,1,0:T(8,128)S(1)}, f32[5,1,96,128]{3,2,1,0:T(8,128)S(1)}, u32[]{:S(2)}, u32[]{:S(2)}) collective-permute-start(f32[5,1,96,128]{3,2,1,0:T(8,128)S(1)} %get-tuple-element.150), channel_id=1, source_target_pairs={{0,1},{1,2},{2,3},{3,4},{4,5},{5,6},{6,7},{8,9},{9,10},{10,11},{11... | collective-permute-start | bytes 737288 | tf_op jit(solution)/shard_map/ppermute | solution.py:25
  186.3 7.5 %collective-permute-start.26 = (f32[5,1,96,128]{3,2,1,0:T(8,128)S(1)}, f32[5,1,96,128]{3,2,1,0:T(8,128)S(1)}, u32[]{:S(2)}, u32[]{:S(2)}) collective-permute-start(f32[5,1,96,128]{3,2,1,0:T(8,128)S(1)} %get-tuple-element.151), channel_id=1, source_target_pairs={{1,0},{2,1},{3,2},{4,3},{5,4},{6,5},{7,6},{9,8},{10,9},{11,10},{12... | collective-permute-start | bytes 737288 | tf_op jit(solution)/shard_map/ppermute | solution.py:27
  (14 other events, 110.1 us)
where the time goes:
time: 198 us; the launch traced here: 196 us
  starting transfers between devices  89.5 us (45%)
  waiting for transfers between devices  58.4 us (29%)
  other arithmetic  34.2 us (17%)
  blocking collectives  6.7 us (3%)
  local copies, waits for them, and re-layouts  6.24 us (3%)
    ppermute x15, starting transfers between devices, with_halo(): lax.ppermute(tail, axis, [(i, (i + 1) % count) for i in range(ends)])  47.8 us
    ppermute x15, waiting for transfers between devices, with_halo(): lax.ppermute(head, axis, [((i + 1) % count, i) for i in range(ends)])  37 us
    ppermute x15, starting transfers between devices, with_halo(): lax.ppermute(head, axis, [((i + 1) % count, i) for i in range(ends)])  33.5 us
    add x8, other arithmetic, relax(): updated = current + damping * freedom * residue / diagonal  12.8 us
    ppermute x3, waiting for transfers between devices, passed_along(): lax.ppermute(value, axis, [(source, source + steps) for source in range(f...  11 us
    ppermute x15, waiting for transfers between devices, with_halo(): lax.ppermute(tail, axis, [(i, (i + 1) % count) for i in range(ends)])  10.4 us
    ppermute x3, starting transfers between devices, passed_along(): lax.ppermute(value, axis, [(source, source + steps) for source in range(f...  8.25 us
    all_gather x1, blocking collectives, on_device(): gathered = lax.all_gather(coarse_rhs, 'tm', axis=0, tiled=True)  6.7 us
  transfers between devices with their start and end apart: 33, of which 23 were waited for; matrix products, arithmetic and copies ran while one was open for 4% of the time, Pallas kernels for 0%

commit v1 on v0

v1 whole, which is shorter than its diff:
```python
import functools

import jax
import jax.numpy as jnp
from jax import lax
from jax.experimental import pallas as pl
from jax.experimental.pallas import tpu as pltpu
from jax.sharding import PartitionSpec as P

PASSES = 4

source_coef = 0.5
drift_coef = 0.5
react_coef = 0.5
damping = 0.8
coarse_lateral = 0.06
coarse_axial = 0.12

PAD = 8


def kernel(
    n_tm,
    n_space,
    regions,
    source,
    initial,
    mobility,
    labels,
    electrode,
    rates,
    out,
    V,
    IE,
    ME,
    EB,
    F,
    FS,
    KP,
    FR,
    FW,
    FX,
    FY,
    BZ,
    AZ,
    D0,
    W,
    TMP,
    HS,
    HX,
    OS,
    OB,
    VO,
    CM,
    GX,
    GY,
    GL,
    GH,
    GD,
    R,
    C,
    UP,
    s_init,
    r_init,
    s_v,
    r_v,
    s_cm,
    r_cm,
    s_hx,
    r_hx,
    s_o,
    r_o,
    s_r,
    r_r,
    s_d,
    r_d,
    s_vo,
    r_vo,
):
    T, X, Y, Z = source.shape
    A, YC = X // 2, Y // 2
    H = -(-n_tm // A)
    E = A * H
    CP = A + 2 * E
    rows = pl.ds(PAD, Y)
    crows = pl.ds(PAD, YC)
    k = lax.axis_index("tm")
    s = lax.axis_index("space")

    def beyond(q, d=1):
        return s >= d if q == 0 else s + d < n_space

    def space_id(q, d=1):
        return {"space": s - d if q == 0 else s + d}

    def remote(src, dst, send, recv, where):
        return pltpu.make_async_remote_copy(
            src_ref=src,
            dst_ref=dst,
            send_sem=send,
            recv_sem=recv,
            device_id=where,
            device_id_type=pl.DeviceIdType.MESH,
        )

    def each_side(action, d=1):
        for q in (0, 1):
            pl.when(beyond(q, d))(functools.partial(action, q))

    barrier = pltpu.get_barrier_semaphore()

    def greet(where):
        pl.semaphore_signal(
            barrier, inc=1, device_id=where, device_id_type=pl.DeviceIdType.MESH
        )

    for d in range(1, H + 1):
        each_side(lambda q, d=d: greet(space_id(q, d)), d)
    for d in range(1, n_tm):
        greet({"tm": lax.rem(k + d, n_tm)})

    edge = jnp.zeros((PAD, Z), jnp.float32)
    plane = jnp.zeros((Y, Z), jnp.float32)
    cplane = jnp.zeros((YC, Z), jnp.float32)
    top, bottom = pl.ds(0, PAD), pl.ds(PAD + Y, PAD)
    ctop, cbottom = pl.ds(0, PAD), pl.ds(PAD + YC, PAD)
    for x in range(X + 2):
        for ref in (IE, ME, W):
            ref[x, top] = edge
            ref[x, bottom] = edge

        def clear(i, carry, x=x):
            for b in (0, 1):
                V[b, i, x, top] = edge
                V[b, i, x, bottom] = edge
            return carry

        lax.fori_loop(1, T + 1, clear, 0)
    for x in range(X):
        FY[x, bottom] = edge
        IE[x + 1, rows] = initial[x]
        ME[x + 1, rows] = mobility[x]
        for b in (0, 1):
            V[b, 0, x + 1, rows] = initial[x]
    W[0, rows] = plane
    W[X + 1, rows] = plane

    def clear_coarse(p, carry):
        for ref in (CM, GY):
            ref[p, ctop] = edge
            ref[p, cbottom] = edge
        for j in range(n_tm):
            C[j, p, ctop] = edge
            C[j, p, cbottom] = edge
        return carry

    lax.fori_loop(0, CP, clear_coarse, 0)
    for q in (0, 1):

        @pl.when(jnp.logical_not(beyond(q)))
        def _(q=q):
            x = 0 if q == 0 else X + 1
            IE[x, rows] = plane
            ME[x, rows] = plane
            FR[x] = plane
            HX[q] = cplane

            def clear_halo(i, carry):
                for b in (0, 1):
                    V[b, i, x, rows] = plane
                return carry

            lax.fori_loop(1, T + 1, clear_halo, 0)

        for d in range(1, H + 1):

            @pl.when(jnp.logical_not(beyond(q, d)))
            def _(q=q, d=d):
                for a in range(A):
                    p = E - A * d + a if q == 0 else E + A * d + a
                    CM[p, crows] = cplane
                    for j in range(n_tm):
                        R[j, p] = cplane

    peers = jnp.minimum(s, H) + jnp.minimum(n_space - 1 - s, H) + (n_tm - 1)
    pl.semaphore_wait(barrier, peers)

    def start_copy(item, q):
        src, dst = ((initial, IE), (mobility, ME), (electrode, EB))[item]
        x = 0 if q == 0 else X - 1
        if item < 2:
            target = dst.at[X + 1 if q == 0 else 0, rows]
        else:
            target = dst.at[1 - q]
        return remote(src.at[x], target, s_init.at[item, q], r_init.at[item, 1 - q], space_id(q))

    def landed(item, q):
        src, dst = ((initial, IE), (mobility, ME), (electrode, EB))[item]
        if item < 2:
            target = dst.at[0 if q == 0 else X + 1, rows]
        else:
            target = dst.at[q]
        return remote(src.at[0], target, s_init.at[item, q], r_init.at[item, q], space_id(q))

    for item in (1, 0, 2):
        each_side(lambda q, item=item: start_copy(item, q).start())

    def pair_rows(value, slot):
        TMP[slot] = value
        return TMP[slot, pl.ds(0, YC, stride=2), :] + TMP[slot, pl.ds(1, YC, stride=2), :]

    for a in range(A):
        CM[E + a, crows] = 0.25 * pair_rows(mobility[2 * a] + mobility[2 * a + 1], a)

    def reach(j, d):
        return min(A, n_tm - j - A * (d - 1))

    def deep(ref, pick, j, q, d, send, recv, incoming):
        n = reach(j, d)
        mine = E if q == 0 else E + A - n
        if incoming:
            there = E - A * d + A - n if q == 0 else E + A * d
        else:
            there = E + A * d if q == 0 else E - A * d + A - n
        slot = 2 * (d - 1)
        return remote(
            pick(ref, mine, n),
            pick(ref, there, n),
            send(slot + q),
            recv(slot + (q if incoming else 1 - q)),
            space_id(q, d),
        )

    def cm_copy(q, d, incoming):
        return deep(
            CM,
            lambda ref, p, n: ref.at[pl.ds(p, n), crows],
            0,
            q,
            d,
            lambda i: s_cm.at[i],
            lambda i: r_cm.at[i],
            incoming,
        )

    for d in range(1, H + 1):
        each_side(lambda q, d=d: cm_copy(q, d, False).start(), d)

    lane = lax.broadcasted_iota(jnp.int32, (Y, Z), 1)
    not_first, not_last = lane > 0, lane < Z - 1

    def half_forcing(t, carry):
        for x in range(X):
            F[t, x] = source_coef * source[t, x]
        return carry

    lax.fori_loop(0, T, half_forcing, 0)
    for x in range(X):
        total = F[0, x]
        for t in range(1, T):
            total = total + F[t, x]
        FS[x] = total
        lab = labels[x]
        rate = jnp.zeros((Y, Z), jnp.float32)
        for i in range(regions):
            rate = jnp.where(lab == i, rates[i], rate)
        KP[x] = rate
        free = 1.0 - electrode[x].astype(jnp.float32)
        FR[x + 1] = free
        FW[x] = damping * free
        mid = mobility[x]
        FY[x, rows] = 0.5 * (mid + ME[x + 1, pl.ds(PAD - 1, Y)])
        FY[x, pl.ds(PAD + Y, 1)] = 0.5 * mobility[x, pl.ds(Y - 1, 1)]
        low = 0.5 * (mid + jnp.where(not_first, pltpu.roll(mid, 1, 1), 0.0))
        high = 0.5 * (mid + jnp.where(not_last, pltpu.roll(mid, Z - 1, 1), 0.0))
        BZ[x] = jnp.where(not_first, (1.0 + drift_coef) * low, 0.0)
        AZ[x] = jnp.where(not_last, high, 0.0)
        D0[x] = 1.0 + low + (1.0 + drift_coef) * high + FY[x, rows] + FY[x, pl.ds(PAD + 1, Y)]
    for x in range(1, X):
        FX[x] = 0.5 * (mobility[x - 1] + mobility[x])

    @pl.when(k == 0)
    def _():
        for a in range(A):
            OB[a] = pair_rows(initial[2 * a] + initial[2 * a + 1], a)

    each_side(lambda q: landed(1, q).wait_recv())
    FX[0] = 0.5 * (ME[0, rows] + ME[1, rows])
    FX[X] = 0.5 * (ME[X, rows] + ME[X + 1, rows])
    for x in range(X):
        D0[x] = D0[x] + FX[x] + FX[x + 1]

    def around(read, x, centre):
        i = x - 1
        return (
            FX[i] * read(x - 1, PAD)
            + FX[i + 1] * read(x + 1, PAD)
            + FY[i, rows] * read(x, PAD - 1)
            + FY[i, pl.ds(PAD + 1, Y)] * read(x, PAD + 1)
            + BZ[i] * pltpu.roll(centre, 1, 1)
            + AZ[i] * pltpu.roll(centre, Z - 1, 1)
        )

    def v_copy(b, t, q):
        x = 1 if q == 0 else X
        there = X + 1 if q == 0 else 0
        return remote(
            V.at[b, t + 1, x, rows],
            V.at[b, t + 1, there, rows],
            s_v.at[b, q, t],
            r_v.at[b, 1 - q, t],
            space_id(q),
        )

    def v_landed(b, t, q):
        x = 0 if q == 0 else X + 1
        return remote(
            V.at[b, t + 1, 1, rows],
            V.at[b, t + 1, x, rows],
            s_v.at[b, q, t],
            r_v.at[b, q, t],
            space_id(q),
        )

    each_side(lambda q: landed(0, q).wait_recv())

    def first_plane(x):
        i = x - 1
        now = IE[x, rows]
        pull = KP[i] * jnp.abs(now)
        diag = D0[i] + pull
        common = around(lambda xx, o: IE[xx, pl.ds(o, Y)], x, now) + now - now * (
            diag - react_coef * pull
        )
        TMP[0] = common
        TMP[1] = FW[i] / diag

        def step(t, carry):
            V[1, t + 1, x, rows] = IE[x, rows] + TMP[1] * (F[t, i] + TMP[0])
            if x in (1, X):
                q = 0 if x == 1 else 1
                pl.when(beyond(q))(lambda: v_copy(1, t, q).start())
            return carry

        lax.fori_loop(0, T, step, 0)

    for x in (1, X) + tuple(range(2, X)):
        first_plane(x)

    def relaxed(b, t, x):
        i = x - 1
        now = V[b, t + 1, x, rows]
        pull = KP[i] * jnp.abs(now)
        diag = D0[i] + pull
        gain = (
            F[t, i]
            + V[b, t, x, rows]
            + around(lambda xx, o: V[b, t + 1, xx, pl.ds(o, Y)], x, now)
            - now * (diag - react_coef * pull)
        )
        return now + FW[i] * gain / diag

    def one_pass(b, arriving, sending, free_send, last):
        o = 1 - b

        def store(t, x, value):
            if last:
                out[t, x - 1] = value
            else:
                V[o, t + 1, x, rows] = value

        def ends(t, carry):
            if arriving:
                each_side(lambda q: v_landed(b, t, q).wait_recv())
            if free_send:
                each_side(lambda q: v_copy(o, t, q).wait_send())
            for q, x in ((0, 1), (1, X)):
                store(t, x, relaxed(b, t, x))
                if sending:
                    pl.when(beyond(q))(functools.partial(lambda q: v_copy(o, t, q).start(), q))
            return carry

        def inner(t, carry):
            for x in range(2, X):
                store(t, x, relaxed(b, t, x))
            return carry

        lax.fori_loop(0, T, ends, 0)
        lax.fori_loop(0, T, inner, 0)

    for number in range(2, PASSES + 1):
        one_pass((number + 1) % 2, True, number < PASSES, number > 2, False)
    g = PASSES % 2

    def total_of(x):
        total = V[g, 1, x, rows]
        for t in range(1, T):
            total = total + V[g, t + 1, x, rows]
        return total

    def hx_copy(q):
        return remote(HS.at[q], HX.at[1 - q], s_hx.at[q], r_hx.at[1 - q], space_id(q))

    def hx_landed(q):
        return remote(HS.at[q], HX.at[q], s_hx.at[q], r_hx.at[q], space_id(q))

    for q, x in ((0, 1), (1, X)):
        total = total_of(x)
        W[x, rows] = total
        HS[q] = 0.25 * pair_rows(FX[0 if q == 0 else X] * total, q)
        pl.when(beyond(q))(functools.partial(lambda q: hx_copy(q).start(), q))

    o_copy = remote(OS, OB, s_o, r_o, {"tm": lax.rem(k + 1, n_tm)})
    for a in range(A):
        OS[a] = pair_rows(V[g, T, 2 * a + 1, rows] + V[g, T, 2 * a + 2, rows], a)

    @pl.when(k < n_tm - 1)
    def _():
        o_copy.start()

    def v_out(t, carry):
        each_side(lambda q: v_copy(g, t, q).start())
        return carry

    lax.fori_loop(0, T, v_out, 0)

    for x in range(2, X):
        W[x, rows] = total_of(x)

    def residual_sum(x):
        i = x - 1
        total = W[x, rows]
        quad = jnp.zeros((Y, Z), jnp.float32)
        for t in range(T):
            value = V[g, t + 1, x, rows]
            quad = quad + value * jnp.abs(value)
        return (
            FS[i]
            + (total - V[g, T, x, rows])
            + around(lambda xx, o: W[xx, pl.ds(o, Y)], x, total)
            - D0[i] * total
            - react_coef * KP[i] * quad
        )

    own = []
    for a in range(A):
        own.append(pair_rows(residual_sum(2 * a + 1) + residual_sum(2 * a + 2), a))

    @pl.when(k > 0)
    def _():
        o_copy.wait_recv()

    each_side(lambda q: hx_landed(q).wait_recv())
    for a in range(A):
        value = 0.25 * (own[a] + OB[a])
        if a == 0:
            value = value + HX[0]
        if a == A - 1:
            value = value + HX[1]
        R[k, E + a] = value

    def r_copy(d):
        return remote(
            R.at[k, pl.ds(E, A)],
            R.at[k, pl.ds(E, A)],
            s_r.at[d],
            r_r.at[k],
            {"tm": lax.rem(k + d, n_tm)},
        )

    def r_landed(j):
        return remote(
            R.at[j, pl.ds(E, A)],
            R.at[j, pl.ds(E, A)],
            s_r.at[0],
            r_r.at[j],
            {"tm": lax.rem(k + 1, n_tm)},
        )

    for d in range(n_tm - 1, 0, -1):
        r_copy(d).start()

    vo_copy = remote(
        V.at[g, T, pl.ds(1, X), rows], VO, s_vo, r_vo, {"tm": lax.rem(k + 1, n_tm)}
    )

    @pl.when(k < n_tm - 1)
    def _():
        vo_copy.start()

    for d in range(1, H + 1):
        each_side(lambda q, d=d: cm_copy(q, d, True).wait_recv(), d)
    clane = lax.broadcasted_iota(jnp.int32, (YC, Z), 1)
    c_first, c_last = clane > 0, clane < Z - 1
    lo = E - (n_tm - 1)
    hi = E + A + (n_tm - 1)

    def coarse_faces(p, carry):
        GX[p] = (0.5 * coarse_lateral) * (CM[p - 1, crows] + CM[p, crows])
        return carry

    lax.fori_loop(lo, hi + 1, coarse_faces, 0)

    def coarse_coefs(p, carry):
        mid = CM[p, crows]
        near = (0.5 * coarse_lateral) * (mid + CM[p, pl.ds(PAD - 1, YC)])
        far = (0.5 * coarse_lateral) * (mid + CM[p, pl.ds(PAD + 1, YC)])
        GY[p, crows] = near
        low = (0.5 * coarse_axial) * (
            mid + jnp.where(c_first, pltpu.roll(mid, 1, 1), 0.0)
        )
        high = (0.5 * coarse_axial) * (
            mid + jnp.where(c_last, pltpu.roll(mid, Z - 1, 1), 0.0)
        )
        GL[p] = jnp.where(c_first, low, 0.0)
        GH[p] = jnp.where(c_last, high, 0.0)
        GD[p] = 1.0 - (GX[p] + GX[p + 1] + near + far + low + high)
        return carry

    lax.fori_loop(lo, hi, coarse_coefs, 0)

    def d_copy(j, q, d, incoming):
        return deep(
            R,
            lambda ref, p, n: ref.at[j, pl.ds(p, n)],
            j,
            q,
            d,
            lambda i: s_d.at[j, i],
            lambda i: r_d.at[j, i],
            incoming,
        )

    def distances(j):
        return [d for d in range(1, H + 1) if reach(j, d) > 0]

    for j in range(n_tm):
        pl.when(k != j)(lambda j=j: r_landed(j).wait_recv())
        for d in distances(j):
            each_side(lambda q, d=d, j=j: d_copy(j, q, d, False).start(), d)

    for j in range(n_tm):
        for d in distances(j):
            each_side(lambda q, d=d, j=j: d_copy(j, q, d, True).wait_recv(), d)

        def coarse_plane(p, carry, j=j):
            if j == 0:
                C[0, p, crows] = R[0, p]
                return carry
            mid = C[j - 1, p, crows]
            value = (
                R[j, p]
                + GD[p] * mid
                + GX[p] * C[j - 1, p - 1, crows]
                + GX[p + 1] * C[j - 1, p + 1, crows]
                + GY[p, crows] * C[j - 1, p, pl.ds(PAD - 1, YC)]
                + GY[p, pl.ds(PAD + 1, YC)] * C[j - 1, p, pl.ds(PAD + 1, YC)]
                + GL[p] * pltpu.roll(mid, 1, 1)
                + GH[p] * pltpu.roll(mid, Z - 1, 1)
            )
            where = A * s + p - E
            inside = jnp.logical_and(where >= 0, where < A * n_space)
            C[j, p, crows] = jnp.where(inside, value, 0.0)
            return carry

        width = n_tm - j
        lax.fori_loop(E - width, E + A + width, coarse_plane, 0)

    each_side(lambda q: landed(2, q).wait_recv())
    for q in (0, 1):

        @pl.when(beyond(q))
        def _(q=q):
            FR[0 if q == 0 else X + 1] = 1.0 - EB[q].astype(jnp.float32)

    def spread(j, x):
        value = C[j, E + (x + 1) // 2 - 1, crows]
        UP[x, pl.ds(0, YC, stride=2), :] = value
        UP[x, pl.ds(1, YC, stride=2), :] = value
        return FR[x] * UP[x]

    def v_home(t, carry):
        each_side(lambda q: v_copy(g, t, q).wait_send())
        each_side(lambda q: v_landed(g, t, q).wait_recv())
        return carry

    lax.fori_loop(0, T, v_home, 0)

    @pl.when(k < n_tm - 1)
    def _():
        vo_copy.wait_send()

    for x in range(X + 2):
        move = spread(k, x)
        for t in range(T):
            V[g, t + 1, x, rows] = V[g, t + 1, x, rows] + move

    @pl.when(k > 0)
    def _():
        vo_copy.wait_recv()
        for x in range(1, X + 1):
            opening = VO[x - 1] + spread(k - 1, x)
            for b in (0, 1):
                V[b, 0, x, rows] = opening

    for number in range(1, PASSES + 1):
        one_pass(
            (g + number + 1) % 2,
            number > 1,
            number < PASSES,
            number in (1, 3),
            number == PASSES,
        )

    def drain(t, carry):
        for b in (0, 1):
            each_side(lambda q, b=b: v_copy(b, t, q).wait_send())
        return carry

    lax.fori_loop(0, T, drain, 0)
    for item in range(3):
        each_side(lambda q, item=item: start_copy(item, q).wait_send())
    each_side(lambda q: hx_copy(q).wait_send())
    for d in range(1, H + 1):
        each_side(lambda q, d=d: cm_copy(q, d, False).wait_send(), d)
    for j in range(n_tm):
        for d in distances(j):
            each_side(lambda q, d=d, j=j: d_copy(j, q, d, False).wait_send(), d)
    for d in range(1, n_tm):
        r_copy(d).wait_send()

    @pl.when(k < n_tm - 1)
    def _():
        o_copy.wait_send()


def solution(mesh):
    n_tm, n_space = mesh.shape["tm"], mesh.shape["space"]

    def on_device(source, initial, mobility, labels, electrode, rates):
        T, X, Y, Z = source.shape
        A, YC = X // 2, Y // 2
        H = -(-n_tm // A)
        CP = A + 2 * A * H
        YP, CYP = Y + 2 * PAD, YC + 2 * PAD
        f32 = jnp.float32
        vm = pltpu.VMEM
        dma = pltpu.SemaphoreType.DMA
        in_vmem = pl.BlockSpec(memory_space=pltpu.VMEM)
        return pl.pallas_call(
            functools.partial(kernel, n_tm, n_space, rates.shape[0]),
            out_shape=jax.ShapeDtypeStruct(source.shape, f32),
            in_specs=[in_vmem] * 5 + [pl.BlockSpec(memory_space=pltpu.SMEM)],
            out_specs=in_vmem,
            scratch_shapes=[
                vm((2, T + 1, X + 2, YP, Z), f32),
                vm((X + 2, YP, Z), f32),
                vm((X + 2, YP, Z), f32),
                vm((2, Y, Z), jnp.int32),
                vm((T, X, Y, Z), f32),
                vm((X, Y, Z), f32),
                vm((X, Y, Z), f32),
                vm((X + 2, Y, Z), f32),
                vm((X, Y, Z), f32),
                vm((X + 1, Y, Z), f32),
                vm((X, YP, Z), f32),
                vm((X, Y, Z), f32),
                vm((X, Y, Z), f32),
                vm((X, Y, Z), f32),
                vm((X + 2, YP, Z), f32),
                vm((max(A, 2), Y, Z), f32),
                vm((2, YC, Z), f32),
                vm((2, YC, Z), f32),
                vm((A, YC, Z), f32),
                vm((A, YC, Z), f32),
                vm((X, Y, Z), f32),
                vm((CP, CYP, Z), f32),
                vm((CP + 1, YC, Z), f32),
                vm((CP, CYP, Z), f32),
                vm((CP, YC, Z), f32),
                vm((CP, YC, Z), f32),
                vm((CP, YC, Z), f32),
                vm((n_tm, CP, YC, Z), f32),
                vm((n_tm, CP, CYP, Z), f32),
                vm((X + 2, Y, Z), f32),
                dma((3, 2)),
                dma((3, 2)),
                dma((2, 2, T)),
                dma((2, 2, T)),
                dma((2 * H,)),
                dma((2 * H,)),
                dma((2,)),
                dma((2,)),
                dma,
                dma,
                dma((n_tm,)),
                dma((n_tm,)),
                dma((n_tm, 2 * H)),
                dma((n_tm, 2 * H)),
                dma,
                dma,
            ],
            compiler_params=pltpu.CompilerParams(
                collective_id=0, has_side_effects=True, vmem_limit_bytes=60 * 2**20
            ),
        )(source, initial, mobility, labels, electrode, rates)

    return jax.shard_map(
        on_device,
        mesh=mesh,
        in_specs=(
            P("tm", "space", None, None),
            P("space", None, None),
            P("space", None, None),
            P("space", None, None),
            P("space", None, None),
            P(),
        ),
        out_specs=P("tm", "space", None, None),
        check_vma=False,
    )
```

time: 198 us -> 47.3 us (0.24); the launches traced: 196 us -> 47.2 us
  starting transfers between devices: 89.5 us -> 0 us
  waiting for transfers between devices: 58.4 us -> 0 us
  Pallas kernels: 0 us -> 45.1 us
  other arithmetic: 34.2 us -> 0 us
  blocking collectives: 6.7 us -> 0 us
  local copies, waits for them, and re-layouts: 6.24 us -> 2.07 us
    ppermute x33 -> x0, starting transfers between devices: 89.5 us -> none  [the longest x15 47.8 us: with_halo(): lax.ppermute(tail, axis, [(i, (i + 1) % count) for i in range(ends)])]
    ppermute x33 -> x0, waiting for transfers between devices: 58.4 us -> none  [the longest x15 37 us: with_halo(): lax.ppermute(head, axis, [((i + 1) % count, i) for i in range(ends)])]
    pallas_call x0 -> x1, Pallas kernels: none -> 45.1 us  [on_device(): pl.pallas_call(functools.partial(kernel, n_tm, n_space, rates.shape[0]),...]
    add x10 -> x0, other arithmetic: 14.3 us -> none  [the longest x8 12.8 us: relax(): updated = current + damping * freedom * residue / diagonal]
    all_gather x1 -> x0, blocking collectives: 6.7 us -> none  [on_device(): gathered = lax.all_gather(coarse_rhs, 'tm', axis=0, tiled=True)]
    dynamic_update_slice x4 -> x0, other arithmetic: 6.43 us -> none  [on_device(): lax.scan(advance, jnp.zeros(gathered.shape[1:], jnp.float32), gathered)]
    reduce_sum x4 -> x0, other arithmetic: 4.52 us -> none  [the longest x2 2.67 us: restrict(): return 0.25 * jnp.sum(grouped, axis=(1, 3, 5))]
    slice x10 -> x0, local copies, waits for them, and re-layouts: 3.39 us -> none  [the longest x5 3.35 us: with_halo(): lax.slice_in_dim(cells, cells.shape[dim] - width, cells.shape[dim], axis=...]
  transfers between devices with their start and end apart: 33 -> 0, of which waited for: 23 -> 0; matrix products, arithmetic and copies ran while one was open for 4% -> 0% of each run, Pallas kernels for 0% -> 0%
where the time goes in v1:
time: 47.3 us; the launch traced here: 47.2 us
  Pallas kernels  45.1 us (95%)
  local copies, waits for them, and re-layouts  2.07 us (4%)
    pallas_call x1, Pallas kernels, on_device(): pl.pallas_call(functools.partial(kernel, n_tm, n_space, rates.shape[0]),...  45.1 us
    unnamed x1, local copies, waits for them, and re-layouts  2.07 us

profile of v1, /device:TPU:13, one launch (start us, length us, event | category | flops | bytes accessed | tf_op | source)
XLA Modules:
  0.0 47.2 jit_solution(2106381858128075802)
XLA Ops:
  0.0 45.1 %shard_map.64 = f32[4,4,96,128]{3,2,1,0:T(8,128)} custom-call(f32[4,4,96,128]{3,2,1,0:T(8,128)} %source.1, f32[4,96,128]{2,1,0:T(8,128)} %initial.1, f32[4,96,128]{2,1,0:T(8,128)} %mobility.1, s32[4,96,128]{2,1,0:T(8,128)} %labels.1, s32[4,96,128]{2,1,0:T(8,128)} %electrode.1, f32[4]{0:T(128)} %rates.1), custom_call_target="tpu_custom_call" | custom-call | tf_op jit(solution)/shard_map/pallas_call | solution.py:650
  45.1 2.1 %copy.8 = f32[4,4,96,128]{3,2,1,0:T(8,128)} copy(f32[4,4,96,128]{3,2,1,0:T(8,128)} %shard_map.64) | data formatting | bytes 1572864

commit v2 on v1

--- a/solution.py
+++ b/solution.py
@@ -17,6 +17,7 @@
 coarse_axial = 0.12
 
 PAD = 8
+CHUNK = 16
 
 
 def kernel(
@@ -41,6 +42,7 @@
     FW,
     FX,
     FY,
+    FZ,
     BZ,
     AZ,
     D0,
@@ -264,7 +266,7 @@
         rate = jnp.zeros((Y, Z), jnp.float32)
         for i in range(regions):
             rate = jnp.where(lab == i, rates[i], rate)
-        KP[x] = rate
+        KP[x] = react_coef * rate
         free = 1.0 - electrode[x].astype(jnp.float32)
         FR[x + 1] = free
         FW[x] = damping * free
@@ -275,6 +277,7 @@
         high = 0.5 * (mid + jnp.where(not_last, pltpu.roll(mid, Z - 1, 1), 0.0))
         BZ[x] = jnp.where(not_first, (1.0 + drift_coef) * low, 0.0)
         AZ[x] = jnp.where(not_last, high, 0.0)
+        FZ[x] = FY[x, pl.ds(PAD + 1, Y)]
         D0[x] = 1.0 + low + (1.0 + drift_coef) * high + FY[x, rows] + FY[x, pl.ds(PAD + 1, Y)]
     for x in range(1, X):
         FX[x] = 0.5 * (mobility[x - 1] + mobility[x])
@@ -290,15 +293,16 @@
     for x in range(X):
         D0[x] = D0[x] + FX[x] + FX[x + 1]
 
-    def around(read, x, centre):
+    def around(read, x, centre, r=0, n=Y):
         i = x - 1
+        here = pl.ds(r, n)
         return (
-            FX[i] * read(x - 1, PAD)
-            + FX[i + 1] * read(x + 1, PAD)
-            + FY[i, rows] * read(x, PAD - 1)
-            + FY[i, pl.ds(PAD + 1, Y)] * read(x, PAD + 1)
-            + BZ[i] * pltpu.roll(centre, 1, 1)
-            + AZ[i] * pltpu.roll(centre, Z - 1, 1)
+            FX[i, here] * read(x - 1, PAD + r)
+            + FX[i + 1, here] * read(x + 1, PAD + r)
+            + FY[i, pl.ds(PAD + r, n)] * read(x, PAD + r - 1)
+            + FZ[i, here] * read(x, PAD + r + 1)
+            + BZ[i, here] * pltpu.roll(centre, 1, 1)
+            + AZ[i, here] * pltpu.roll(centre, Z - 1, 1)
         )
 
     def v_copy(b, t, q):
@@ -327,13 +331,11 @@
     def first_plane(x):
         i = x - 1
         now = IE[x, rows]
-        pull = KP[i] * jnp.abs(now)
-        diag = D0[i] + pull
-        common = around(lambda xx, o: IE[xx, pl.ds(o, Y)], x, now) + now - now * (
-            diag - react_coef * pull
-        )
+        half = KP[i] * jnp.abs(now)
+        part = D0[i] + half
+        common = around(lambda xx, o: IE[xx, pl.ds(o, Y)], x, now) + now - now * part
         TMP[0] = common
-        TMP[1] = FW[i] / diag
+        TMP[1] = FW[i] / (part + half)
 
         def step(t, carry):
             V[1, t + 1, x, rows] = IE[x, rows] + TMP[1] * (F[t, i] + TMP[0])
@@ -347,46 +349,44 @@
     for x in (1, X) + tuple(range(2, X)):
         first_plane(x)
 
-    def relaxed(b, t, x):
+    def relaxed(b, t, x, r, n):
         i = x - 1
-        now = V[b, t + 1, x, rows]
-        pull = KP[i] * jnp.abs(now)
-        diag = D0[i] + pull
+        here, mine = pl.ds(r, n), pl.ds(PAD + r, n)
+        now = V[b, t + 1, x, mine]
+        half = KP[i, here] * jnp.abs(now)
+        part = D0[i, here] + half
         gain = (
-            F[t, i]
-            + V[b, t, x, rows]
-            + around(lambda xx, o: V[b, t + 1, xx, pl.ds(o, Y)], x, now)
-            - now * (diag - react_coef * pull)
-        )
-        return now + FW[i] * gain / diag
+            around(lambda xx, o: V[b, t + 1, xx, pl.ds(o, n)], x, now, r, n)
+            + (F[t, i, here] + V[b, t, x, mine])
+            - now * part
+        )
+        return now + FW[i, here] * gain / (part + half)
 
     def one_pass(b, arriving, sending, free_send, last):
         o = 1 - b
 
-        def store(t, x, value):
-            if last:
-                out[t, x - 1] = value
-            else:
-                V[o, t + 1, x, rows] = value
-
-        def ends(t, carry):
+        def store(t, x):
+            for r in range(0, Y, CHUNK):
+                value = relaxed(b, t, x, r, CHUNK)
+                if last:
+                    out[t, x - 1, pl.ds(r, CHUNK)] = value
+                else:
+                    V[o, t + 1, x, pl.ds(PAD + r, CHUNK)] = value
+
+        def step(t, carry):
             if arriving:
                 each_side(lambda q: v_landed(b, t, q).wait_recv())
             if free_send:
                 each_side(lambda q: v_copy(o, t, q).wait_send())
             for q, x in ((0, 1), (1, X)):
-                store(t, x, relaxed(b, t, x))
-                if sending:
-                    pl.when(beyond(q))(functools.partial(lambda q: v_copy(o, t, q).start(), q))
+                store(t, x)
+            if sending:
+                each_side(lambda q: v_copy(o, t, q).start())
+            for x in range(2, X):
+                store(t, x)
             return carry
 
-        def inner(t, carry):
-            for x in range(2, X):
-                store(t, x, relaxed(b, t, x))
-            return carry
-
-        lax.fori_loop(0, T, ends, 0)
-        lax.fori_loop(0, T, inner, 0)
+        lax.fori_loop(0, T, step, 0)
 
     for number in range(2, PASSES + 1):
         one_pass((number + 1) % 2, True, number < PASSES, number > 2, False)
@@ -439,7 +439,7 @@
             + (total - V[g, T, x, rows])
             + around(lambda xx, o: W[xx, pl.ds(o, Y)], x, total)
             - D0[i] * total
-            - react_coef * KP[i] * quad
+            - KP[i] * quad
         )
 
     own = []
@@ -564,7 +564,7 @@
             return carry
 
         width = n_tm - j
-        lax.fori_loop(E - width, E + A + width, coarse_plane, 0)
+        lax.fori_loop(E - width, E + A + width, coarse_plane, 0, unroll=2)
 
     each_side(lambda q: landed(2, q).wait_recv())
     for q in (0, 1):
@@ -664,6 +664,7 @@
                 vm((X, Y, Z), f32),
                 vm((X + 1, Y, Z), f32),
                 vm((X, YP, Z), f32),
+                vm((X, Y, Z), f32),
                 vm((X, Y, Z), f32),
                 vm((X, Y, Z), f32),
                 vm((X, Y, Z), f32),

time: 47.3 us -> 45.8 us (0.968)
  Pallas kernels: 45.1 us -> 43.5 us
    pallas_call x1, Pallas kernels: 45.1 us -> 43.5 us  [on_device(): pl.pallas_call(functools.partial(kernel, n_tm, n_space, rates.shape[0]),...]
where the time goes in v2:
time: 45.8 us; the launch traced here: 45.6 us
  Pallas kernels  43.5 us (95%)
  local copies, waits for them, and re-layouts  2.07 us (5%)
    pallas_call x1, Pallas kernels, on_device(): pl.pallas_call(functools.partial(kernel, n_tm, n_space, rates.shape[0]),...  43.5 us
    unnamed x1, local copies, waits for them, and re-layouts  2.07 us

profile of v2, /device:TPU:13, one launch (start us, length us, event | category | flops | bytes accessed | tf_op | source)
XLA Modules:
  0.0 45.6 jit_solution(5201404442354738806)
XLA Ops:
  0.0 43.5 %shard_map.64 = f32[4,4,96,128]{3,2,1,0:T(8,128)} custom-call(f32[4,4,96,128]{3,2,1,0:T(8,128)} %source.1, f32[4,96,128]{2,1,0:T(8,128)} %initial.1, f32[4,96,128]{2,1,0:T(8,128)} %mobility.1, s32[4,96,128]{2,1,0:T(8,128)} %labels.1, s32[4,96,128]{2,1,0:T(8,128)} %electrode.1, f32[4]{0:T(128)} %rates.1), custom_call_target="tpu_custom_call" | custom-call | tf_op jit(solution)/shard_map/pallas_call | solution.py:650
  43.5 2.1 %copy.8 = f32[4,4,96,128]{3,2,1,0:T(8,128)} copy(f32[4,4,96,128]{3,2,1,0:T(8,128)} %shard_map.64) | data formatting | bytes 1572864
